TPU v7x, 128 devices: a whole 4x4x4 slice. The times are simulated.
128 devices in a mesh: grp: 4 (over z), tile: 32 (over y, x, core).
Axes of the slice: x: 4, y: 4, z: 4, core: 2. Of those that a mesh axis runs over, the one named last changes fastest.
Arguments:
- right_side: float32 [16, 32768], P(None, ('grp', 'tile')), may hold values from -6 to 6
- ridge: float32 [32768], P(('grp', 'tile')), may hold values from 1 to 4
- tiles: float32 [512, 1024, 1024], P(('grp', 'tile')), may hold values from -0.013671875 to 0.013671875
- tile_list: int32 [512, 2], P(('grp', 'tile')), may hold values from 0 to 31, as said below
Outputs:
- solution: float32 [16, 32768], P(None, ('grp', 'tile'))
- residual: float32 [16, 32768], P(None, ('grp', 'tile'))
Inputs may be any that keep to these rules, and one draw needn't show every extreme that they name: `tile_list`: each row is a pair (row block, column block) with row block >= column block; no pair appears twice; rows stand in packed row-major order (row block rising, then column block rising).
All inputs are finite; a program needn't handle non-finite values.
Results may differ from a plain program's by a relative error of at most 0.0003.
Values sent between devices are 32-bit elements; how exact they have to be, the bound alone decides.
No kernel may reach another device: no remote copies, remote signals or barrier semaphores. Data moves between devices by JAX's collectives and lax.ppermute only.
A program may use at most 64 MiB of HBM per device.

v0:
```python
import jax
import jax.numpy as jnp
from jax import lax
from jax.sharding import PartitionSpec as P

ITERS = 2


def gauss_solve(matrix, rhs):
    order = matrix.shape[0]
    for pivot in range(order):
        scale = 1.0 / matrix[pivot, pivot]
        row_new = matrix[pivot] * scale
        rhs_new = rhs[pivot] * scale
        factor = matrix[:, pivot] * (1.0 - (jnp.arange(order) == pivot).astype(matrix.dtype))
        matrix = matrix - factor[:, None] * row_new[None, :]
        rhs = rhs - factor[:, None] * rhs_new[None, :]
        matrix = matrix.at[pivot].set(row_new)
        rhs = rhs.at[pivot].set(rhs_new)
    return rhs


def gram(left, right):
    return lax.dot_general(
        left,
        right,
        (((1,), (1,)), ((), ())),
        precision=lax.Precision.HIGHEST,
        preferred_element_type=jnp.float32,
    )


def mixed(coeffs, rows):
    return jnp.dot(coeffs.T, rows, precision=lax.Precision.HIGHEST)


def tile_masks(order):
    rowid = lax.broadcasted_iota(jnp.int32, (order, order), 0)
    colid = lax.broadcasted_iota(jnp.int32, (order, order), 1)
    return (rowid >= colid, rowid > colid)


def apply_kernel(tiles, tile_list, field):
    order = tiles.shape[1]
    lower, strict = tile_masks(order)

    def step(total, item):
        tile, pair = item
        block_row = pair[0]
        block_col = pair[1]
        differ = block_row != block_col
        direct_tile = jnp.where(jnp.logical_or(lower, differ), tile, jnp.zeros_like(tile))
        mirror_tile = jnp.where(jnp.logical_or(strict, differ), tile, jnp.zeros_like(tile))
        row_start = block_row * order
        col_start = block_col * order
        from_col = lax.dynamic_slice_in_dim(field, col_start, order, 1)
        from_row = lax.dynamic_slice_in_dim(field, row_start, order, 1)
        into_row = lax.dot_general(
            from_col,
            direct_tile,
            (((1,), (1,)), ((), ())),
            precision=lax.Precision.HIGHEST,
            preferred_element_type=jnp.float32,
        )
        into_col = jnp.dot(
            from_row,
            mirror_tile,
            precision=lax.Precision.HIGHEST,
            preferred_element_type=jnp.float32,
        )
        total = lax.dynamic_update_slice_in_dim(
            total, lax.dynamic_slice_in_dim(total, row_start, order, 1) + into_row, row_start, 1
        )
        total = lax.dynamic_update_slice_in_dim(
            total, lax.dynamic_slice_in_dim(total, col_start, order, 1) + into_col, col_start, 1
        )
        return (total, None)

    start = jnp.zeros(field.shape, jnp.float32)
    total, _ = lax.scan(step, start, (tiles, tile_list))
    return total


def local(right_side, ridge, tiles, tile_list):
    solution = jnp.zeros_like(right_side)
    residual = right_side
    direction = right_side
    norm_now = lax.psum(gram(residual, residual), ("grp", "tile"))
    for step in range(ITERS):
        whole_direction = lax.all_gather(direction, ("grp", "tile"), axis=1, tiled=True)
        partial_image = apply_kernel(tiles, tile_list, whole_direction)
        image = (
            lax.psum_scatter(partial_image, ("grp", "tile"), scatter_dimension=1, tiled=True)
            + ridge[None, :] * direction
        )
        curvature = lax.psum(gram(direction, image), ("grp", "tile"))
        alpha = gauss_solve(curvature, norm_now)
        solution = solution + mixed(alpha, direction)
        residual = residual - mixed(alpha, image)
        if step + 1 < ITERS:
            norm_next = lax.psum(gram(residual, residual), ("grp", "tile"))
            beta = gauss_solve(norm_now, norm_next)
            direction = residual + mixed(beta, direction)
            norm_now = norm_next
    return (solution, residual)


def solution(mesh):
    return jax.shard_map(
        local,
        mesh=mesh,
        in_specs=(
            P(None, ("grp", "tile")),
            P(("grp", "tile")),
            P(("grp", "tile"), None, None),
            P(("grp", "tile"), None),
        ),
        out_specs=(P(None, ("grp", "tile")), P(None, ("grp", "tile"))),
        check_vma=False,
    )
```

profile of v0, /device:TPU:1, one launch (start us, length us, event | category | flops | bytes accessed | tf_op | source)
XLA Modules:
  0.0 1806.4 jit_solution(17161838119397110656)
XLA Ops:
  7.9 71.4 %all-gather.3.cloned.1.call-done = f32[16,32768]{1,0:T(8,128)} async-done(((f32[16,256]{1,0:T(8,128)}), f32[16,32768]{1,0:T(8,128)}) %all-gather.3.cloned.1.call-update) | async-done | bytes 2097168 | tf_op jit(solution)/shard_map/all_gather | solution.py:90
  79.5 55.9 %while.115 = (s32[]{:T(128)}, f32[16,32768]{1,0:T(8,128)S(1)}, s32[4,2]{0,1:T(2,128)}, f32[16,32768]{1,0:T(8,128)}, f32[4,1024,1024]{2,1,0:T(8,128)}, /*index=5*/s32[]{:T(128)}, s32[1,1]{0,1:T(1,128)}, s32[]{:T(128)}, s32[]{:T(128)}) while((s32[]{:T(128)}, f32[16,32768]{1,0:T(8,128)S(1)}, s32[4,2]{0,1:T(2,128)}, ...), condition=%wide.region_2.3_spmd.clone, body=%wide.region_1.2_spmd.clone.sunk | while | flops 408977408 | bytes 8784118 | solution.py:80
  83.4 5.6 fusion.227
  89.0 4.5 fusion.228
  97.3 5.6 fusion.227
  103.0 4.5 fusion.228
  111.3 5.6 fusion.227
  116.9 4.5 fusion.228
  125.3 5.6 fusion.227
  130.9 4.5 fusion.228
  137.0 630.1 %reduce-scatter.3.cloned.1.call-done = f32[16,256]{1,0:T(8,128)} async-done(((f32[16,32768]{1,0:T(8,128)}), f32[16,256]{1,0:T(8,128)}) %reduce-scatter.3.cloned.1.call-update) | async-done | bytes 16400 | tf_op jit(solution)/shard_map/reduce_scatter | solution.py:93
  767.9 69.3 %all-reduce = (f32[16,16]{1,0:T(8,128)S(1)}, f32[16,16]{1,0:T(8,128)S(1)}) all-reduce(f32[16,16]{1,0:T(8,128)S(1)} %fusion.107, f32[16,16]{1,0:T(8,128)S(1)} %convolution_bitcast_fusion), channel_id=1, replica_groups=mesh['grp'=4,'tile'=32] {'grp','tile'}, use_global_device_ids=true, to_apply=%region_0.0 | all-reduce | flops 512 | bytes 4096 | tf_op jit(solution)/shard_map/psum | solution.py:88
  865.5 62.7 %psum.30 = f32[16,16]{1,0:T(8,128)S(1)} all-reduce(f32[16,16]{1,0:T(8,128)S(1)} %fusion.109), channel_id=1, replica_groups=mesh['grp'=4,'tile'=32] {'grp','tile'}, use_global_device_ids=true, to_apply=%region_5.6 | all-reduce | flops 256 | bytes 2048 | tf_op jit(solution)/shard_map/psum | solution.py:101
  954.0 62.6 %all-gather.5.cloned.1.call-done = f32[16,32768]{1,0:T(8,128)} async-done(((f32[16,256]{1,0:T(8,128)}), f32[16,32768]{1,0:T(8,128)}) %all-gather.5.cloned.1.call-update) | async-done | bytes 2097168 | tf_op jit(solution)/shard_map/all_gather | solution.py:90
  1016.8 52.9 %while.116 = (s32[]{:T(128)}, f32[16,32768]{1,0:T(8,128)S(1)}, s32[4,2]{0,1:T(2,128)S(1)}, f32[16,32768]{1,0:T(8,128)}, f32[4,1024,1024]{2,1,0:T(8,128)}, /*inde...) while((s32[]{:T(128)}, f32[16,32768]{1,0:T(8,128)S(1)}, s32[4,2]{0,1:T(2,128)S(1)}, ...), condition=%wide.region_7.8_spmd.clone, body=%wide.region_6.7_spmd.clone.sunk | while | flops 408977408 | bytes 8784118 | solution.py:80
  1019.9 5.6 fusion.232
  1025.5 4.5 fusion.233
  1033.1 5.6 fusion.232
  1038.7 4.5 fusion.233
  1046.3 5.6 fusion.232
  1059.6 5.6 fusion.232
  1065.2 4.5 fusion.233
  1071.3 630.1 %reduce-scatter.5.cloned.1.call-done = f32[16,256]{1,0:T(8,128)} async-done(((f32[16,32768]{1,0:T(8,128)}), f32[16,256]{1,0:T(8,128)}) %reduce-scatter.5.cloned.1.call-update) | async-done | bytes 16400 | tf_op jit(solution)/shard_map/reduce_scatter | solution.py:93
  1702.2 69.2 %psum.31 = f32[16,16]{1,0:T(8,128)S(1)} all-reduce(f32[16,16]{1,0:T(8,128)S(1)} %fusion.52), channel_id=1, replica_groups=mesh['grp'=4,'tile'=32] {'grp','tile'}, use_global_device_ids=true, to_apply=%region_9.10 | all-reduce | flops 256 | bytes 2048 | tf_op jit(solution)/shard_map/psum | solution.py:96
  (465 shorter events, 66.1 us)
Async XLA Ops:
  7.2 72.2 %all-gather.3.cloned.1.call-start = ((), (), s32[]{:S(2)}) async-start(), calls=%async_computation.2 | async-start | bytes 2113536 | tf_op jit(solution)/shard_map/all_gather | solution.py:90
  7.9 759.1 %reduce-scatter.3.cloned.1.call-start = ((), (), s32[]{:S(2)}) async-start(), calls=%async_computation.3 | async-start | bytes 2113536 | tf_op jit(solution)/shard_map/reduce_scatter | solution.py:93
  79.5 57.3 %copy-start.2 = (f32[16,256]{1,0:T(8,128)S(1)}, f32[16,256]{1,0:T(8,128)}, u32[]{:S(2)}) copy-start(f32[16,256]{1,0:T(8,128)} %param.194) | copy-start | bytes 49156
  79.5 687.5 %copy-start.5 = (f32[256]{0:T(256)S(1)}, f32[256]{0:T(256)}, u32[]{:S(2)}) copy-start(f32[256]{0:T(256)} %param.195) | copy-start | bytes 3076
  135.4 1.4 copy-start.1
  135.4 881.3 %copy-start.4 = (s32[4,2]{0,1:T(2,128)S(1)}, s32[4,2]{0,1:T(2,128)}, u32[]{:S(2)}) copy-start(s32[4,2]{0,1:T(2,128)} %get-tuple-element.1476) | copy-start | bytes 100
  136.8 879.8 %all-gather.5.cloned.1.call-start = ((), (), s32[]{:S(2)}) async-start(), calls=%async_computation.4 | async-start | bytes 2113536 | tf_op jit(solution)/shard_map/all_gather | solution.py:90
  953.9 747.5 %reduce-scatter.5.cloned.1.call-start = ((), (), s32[]{:S(2)}) async-start(), calls=%async_computation.5 | async-start | bytes 2113536 | tf_op jit(solution)/shard_map/reduce_scatter | solution.py:93
  1016.8 684.6 %copy-start.3 = (f32[16,256]{1,0:T(8,128)S(1)}, f32[16,256]{1,0:T(8,128)}, u32[]{:S(2)}) copy-start(f32[16,256]{1,0:T(8,128)} %convolution_add_fusion.1) | copy-start | bytes 49156
  1069.7 1.4 copy-start
Sparse Core Ops, SparseCore 0:
  10.8 68.4 all-gather.2
  136.9 630.0 reduce-scatter.2
  954.1 62.5 all-gather.4
  1071.2 630.1 reduce-scatter.4
where the time goes:
time: 1810 us
  waiting for transfers between devices  1390 us (77%)
  blocking collectives  201 us (11%)
  matrix products  87.4 us (5%)
  between operations  48.2 us (3%)
  local copies, waits for them, and re-layouts  41.3 us (2%)
  loops' own time  20 us (1%)
    reduce_scatter x2, waiting for transfers between devices, local(): lax.psum_scatter(partial_image, ('grp', 'tile'), scatter_dimension=1, til...  1260 us
    all_gather x2, waiting for transfers between devices, local(): lax.all_gather(direction, ('grp', 'tile'), axis=1, tiled=True)  134 us
    psum x1, blocking collectives, local(): norm_now = lax.psum(gram(residual, residual), ('grp', 'tile'))  69.3 us
    psum x1, blocking collectives, local(): curvature = lax.psum(gram(direction, image), ('grp', 'tile'))  69.2 us
    psum x1, blocking collectives, local(): norm_next = lax.psum(gram(residual, residual), ('grp', 'tile'))  62.7 us
    dot_general x8, matrix products, step(): lax.dot_general(from_col, direct_tile, (((1,), (1,)), ((), ())), precisio...  45.1 us
  transfers between devices with their start and end apart: 4, of which 4 were waited for; matrix products, arithmetic and copies ran while one was open for 0% of the time, Pallas kernels for 0%

commit v1 on v0

--- a/solution.py
+++ b/solution.py
@@ -85,7 +85,7 @@
     solution = jnp.zeros_like(right_side)
     residual = right_side
     direction = right_side
-    norm_now = lax.psum(gram(residual, residual), ("grp", "tile"))
+    norm_now = lax.psum(lax.psum(gram(residual, residual), "tile"), "grp")
     for step in range(ITERS):
         whole_direction = lax.all_gather(direction, ("grp", "tile"), axis=1, tiled=True)
         partial_image = apply_kernel(tiles, tile_list, whole_direction)

time: 1810 us -> 1810 us (level)
  blocking collectives: 201 us -> 271 us
  waiting for transfers between devices: 1390 us -> 1320 us
    reduce_scatter x2, waiting for transfers between devices: 1260 us -> 1190 us  [local(): lax.psum_scatter(partial_image, ('grp', 'tile'), scatter_dimension=1, til...]
    psum x1 -> x2, blocking collectives: 69.2 us -> 138 us  [local(): curvature = lax.psum(gram(direction, image), ('grp', 'tile'))]
    psum x1 -> x2, blocking collectives: 69.3 us -> 70.4 us  [local(): norm_now = lax.psum(lax.psum(gram(residual, residual), 'tile'), 'grp')]
where the time goes in v1:
time: 1810 us
  waiting for transfers between devices  1320 us (73%)
  blocking collectives  271 us (15%)
  matrix products  87.4 us (5%)
  between operations  48.2 us (3%)
  local copies, waits for them, and re-layouts  41.3 us (2%)
  loops' own time  20 us (1%)
    reduce_scatter x2, waiting for transfers between devices, local(): lax.psum_scatter(partial_image, ('grp', 'tile'), scatter_dimension=1, til...  1190 us
    psum x2, blocking collectives, local(): curvature = lax.psum(gram(direction, image), ('grp', 'tile'))  138 us
    all_gather x2, waiting for transfers between devices, local(): lax.all_gather(direction, ('grp', 'tile'), axis=1, tiled=True)  134 us
    psum x2, blocking collectives, local(): norm_now = lax.psum(lax.psum(gram(residual, residual), 'tile'), 'grp')  70.4 us
    psum x1, blocking collectives, local(): norm_next = lax.psum(gram(residual, residual), ('grp', 'tile'))  62.7 us
    dot_general x8, matrix products, step(): lax.dot_general(from_col, direct_tile, (((1,), (1,)), ((), ())), precisio...  45.1 us
  transfers between devices with their start and end apart: 4, of which 4 were waited for; matrix products, arithmetic and copies ran while one was open for 0% of the time, Pallas kernels for 0%

profile of v1, /device:TPU:1, one launch (start us, length us, event | category | flops | bytes accessed | tf_op | source)
XLA Modules:
  0.0 1806.2 jit_solution(15185285936068943812)
XLA Ops:
  7.9 71.4 %all-gather.3.cloned.1.call-done = f32[16,32768]{1,0:T(8,128)} async-done(((f32[16,256]{1,0:T(8,128)}), f32[16,32768]{1,0:T(8,128)}) %all-gather.3.cloned.1.call-update) | async-done | bytes 2097168 | tf_op jit(solution)/shard_map/all_gather | solution.py:90
  79.5 55.9 %while.115 = (s32[]{:T(128)}, f32[16,32768]{1,0:T(8,128)S(1)}, s32[4,2]{0,1:T(2,128)}, f32[16,32768]{1,0:T(8,128)}, f32[4,1024,1024]{2,1,0:T(8,128)}, /*index=5*/s32[]{:T(128)}, s32[1,1]{0,1:T(1,128)}, s32[]{:T(128)}, s32[]{:T(128)}) while((s32[]{:T(128)}, f32[16,32768]{1,0:T(8,128)S(1)}, s32[4,2]{0,1:T(2,128)}, ...), condition=%wide.region_3.4_spmd.clone, body=%wide.region_2.3_spmd.clone.sunk | while | flops 408977408 | bytes 8784118 | solution.py:80
  83.4 5.6 fusion.226
  89.0 4.5 fusion.227
  97.3 5.6 fusion.226
  103.0 4.5 fusion.227
  111.3 5.6 fusion.226
  116.9 4.5 fusion.227
  125.3 5.6 fusion.226
  130.9 4.5 fusion.227
  137.0 63.3 %psum.35 = f32[16,16]{1,0:T(8,128)S(1)} all-reduce(f32[16,16]{1,0:T(8,128)S(1)} %fusion.107), channel_id=1, replica_groups=mesh['grp'=4,'tile'=32] {'tile'}, use_global_device_ids=true, to_apply=%region_0.0 | all-reduce | flops 256 | bytes 2048 | tf_op jit(solution)/shard_map/psum | solution.py:88
  200.3 7.1 psum.36
  208.7 559.7 %reduce-scatter.3.cloned.1.call-done = f32[16,256]{1,0:T(8,128)} async-done(((f32[16,32768]{1,0:T(8,128)}), f32[16,256]{1,0:T(8,128)}) %reduce-scatter.3.cloned.1.call-update) | async-done | bytes 16400 | tf_op jit(solution)/shard_map/reduce_scatter | solution.py:93
  769.3 69.1 %psum.37 = f32[16,16]{1,0:T(8,128)S(1)} all-reduce(f32[16,16]{1,0:T(8,128)S(1)} %convolution_bitcast_fusion), channel_id=1, replica_groups=mesh['grp'=4,'tile'=32] {'grp','tile'}, use_global_device_ids=true, to_apply=%region_5.6 | all-reduce | flops 256 | bytes 2048 | tf_op jit(solution)/shard_map/psum | solution.py:96
  865.5 62.7 %psum.38 = f32[16,16]{1,0:T(8,128)S(1)} all-reduce(f32[16,16]{1,0:T(8,128)S(1)} %fusion.109), channel_id=1, replica_groups=mesh['grp'=4,'tile'=32] {'grp','tile'}, use_global_device_ids=true, to_apply=%region_6.7 | all-reduce | flops 256 | bytes 2048 | tf_op jit(solution)/shard_map/psum | solution.py:101
  953.9 62.5 %all-gather.5.cloned.1.call-done = f32[16,32768]{1,0:T(8,128)} async-done(((f32[16,256]{1,0:T(8,128)}), f32[16,32768]{1,0:T(8,128)}) %all-gather.5.cloned.1.call-update) | async-done | bytes 2097168 | tf_op jit(solution)/shard_map/all_gather | solution.py:90
  1016.6 52.9 %while.116 = (s32[]{:T(128)}, f32[16,32768]{1,0:T(8,128)S(1)}, s32[4,2]{0,1:T(2,128)S(1)}, f32[16,32768]{1,0:T(8,128)}, f32[4,1024,1024]{2,1,0:T(8,128)}, /*inde...) while((s32[]{:T(128)}, f32[16,32768]{1,0:T(8,128)S(1)}, s32[4,2]{0,1:T(2,128)S(1)}, ...), condition=%wide.region_8.9_spmd.clone, body=%wide.region_7.8_spmd.clone.sunk | while | flops 408977408 | bytes 8784118 | solution.py:80
  1019.7 5.6 fusion.231
  1032.9 5.6 fusion.231
  1038.5 4.5 fusion.232
  1046.1 5.6 fusion.231
  1059.3 5.6 fusion.231
  1071.1 630.1 %reduce-scatter.5.cloned.1.call-done = f32[16,256]{1,0:T(8,128)} async-done(((f32[16,32768]{1,0:T(8,128)}), f32[16,256]{1,0:T(8,128)}) %reduce-scatter.5.cloned.1.call-update) | async-done | bytes 16400 | tf_op jit(solution)/shard_map/reduce_scatter | solution.py:93
  1702.0 69.2 %psum.39 = f32[16,16]{1,0:T(8,128)S(1)} all-reduce(f32[16,16]{1,0:T(8,128)S(1)} %fusion.52), channel_id=1, replica_groups=mesh['grp'=4,'tile'=32] {'grp','tile'}, use_global_device_ids=true, to_apply=%region_10.11 | all-reduce | flops 256 | bytes 2048 | tf_op jit(solution)/shard_map/psum | solution.py:96
  (467 shorter events, 75.2 us)
Async XLA Ops:
  7.2 72.2 %all-gather.3.cloned.1.call-start = ((), (), s32[]{:S(2)}) async-start(), calls=%async_computation.2 | async-start | bytes 2113536 | tf_op jit(solution)/shard_map/all_gather | solution.py:90
  7.9 760.5 %reduce-scatter.3.cloned.1.call-start = ((), (), s32[]{:S(2)}) async-start(), calls=%async_computation.3 | async-start | bytes 2113536 | tf_op jit(solution)/shard_map/reduce_scatter | solution.py:93
  79.5 57.3 %copy-start.2 = (f32[16,256]{1,0:T(8,128)S(1)}, f32[16,256]{1,0:T(8,128)}, u32[]{:S(2)}) copy-start(f32[16,256]{1,0:T(8,128)} %param.194) | copy-start | bytes 49156
  79.5 688.9 %copy-start.5 = (f32[256]{0:T(256)S(1)}, f32[256]{0:T(256)}, u32[]{:S(2)}) copy-start(f32[256]{0:T(256)} %param.195) | copy-start | bytes 3076
  135.4 1.4 copy-start.1
  135.4 881.1 %copy-start.4 = (s32[4,2]{0,1:T(2,128)S(1)}, s32[4,2]{0,1:T(2,128)}, u32[]{:S(2)}) copy-start(s32[4,2]{0,1:T(2,128)} %get-tuple-element.1473) | copy-start | bytes 100
  136.8 879.6 %all-gather.5.cloned.1.call-start = ((), (), s32[]{:S(2)}) async-start(), calls=%async_computation.4 | async-start | bytes 2113536 | tf_op jit(solution)/shard_map/all_gather | solution.py:90
  953.9 747.3 %reduce-scatter.5.cloned.1.call-start = ((), (), s32[]{:S(2)}) async-start(), calls=%async_computation.5 | async-start | bytes 2113536 | tf_op jit(solution)/shard_map/reduce_scatter | solution.py:93
  1016.6 684.6 %copy-start.3 = (f32[16,256]{1,0:T(8,128)S(1)}, f32[16,256]{1,0:T(8,128)}, u32[]{:S(2)}) copy-start(f32[16,256]{1,0:T(8,128)} %convolution_add_fusion.1) | copy-start | bytes 49156
  1069.5 1.4 copy-start
Sparse Core Ops, SparseCore 0:
  10.8 68.4 all-gather.2
  136.9 631.4 reduce-scatter.2
  954.0 62.3 all-gather.4
  1071.0 630.1 reduce-scatter.4
